TPU v7x, 256 devices: a whole 4x4x8 slice. The times are simulated.
256 devices in a mesh: gx: 4 (over y), gy: 16 (over z, core), gz: 4 (over x).
Axes of the slice: x: 4, y: 4, z: 8, core: 2. Of those that a mesh axis runs over, the one named last changes fastest.
Arguments:
- flux_jacobian_factor: bfloat16 [4, 64, 8, 320, 320], P('gx', 'gy', 'gz'), may hold values from -6 to 6
- mass_over_timestep: float32 [4, 64, 8, 320], P('gx', 'gy', 'gz'), may hold values from 0.5 to 2
- face_jacobian: float32 [4, 64, 8, 3, 80, 160], P('gx', 'gy', 'gz'), may hold values from -1 to 1
- face_flags: int32 [4, 64, 8, 6], P('gx', 'gy', 'gz'), may hold values from 0 to 1, as said below
- right_side: float32 [4, 64, 8, 320], P('gx', 'gy', 'gz'), may hold values from -36 to 36
Outputs:
- update: float32 [4, 64, 8, 320], P('gx', 'gy', 'gz')
Inputs may be any that keep to these rules, and one draw needn't show every extreme that they name: face_flags[e, 2 d] and face_flags[e, 2 d + 1] mark the lower and upper face of element e along dimension d as a wall (1) or open (0); the upper flag of an element along a dimension equals the lower flag of the element after it along that dimension.
All inputs are finite; a program needn't handle non-finite values.
Results may differ from a plain program's by a relative error of at most 0.0003.
Values sent between devices are 32-bit elements; how exact they have to be, the bound alone decides.
No kernel may reach another device: no remote copies, remote signals or barrier semaphores. Data moves between devices by JAX's collectives and lax.ppermute only.
A program may use at most 128 MiB of HBM per device.

v0:
```python
import jax
import jax.numpy as jnp
from jax import lax
from jax.sharding import PartitionSpec as P

VARS = 5
ORDER = 4
KRYLOV = 3
ELEMENT_UNKNOWNS = 320
FACE_UNKNOWNS = 80
full_precision = lax.Precision.HIGHEST
wall_weight = 0.5


def passed_along(block, axis, distance):
    devices = range(lax.axis_size(axis))
    route = [(i - distance, i) for i in devices if i - distance in devices]
    return lax.ppermute(block, axis, route)


def padded_2(cells, sides, width):
    for axis, dim in sides:
        count = lax.axis_size(axis)
        ends = count - 1
        head = lax.slice_in_dim(cells, 0, width, axis=dim)
        tail = lax.slice_in_dim(cells, cells.shape[dim] - width, cells.shape[dim], axis=dim)
        cells = jnp.concatenate(
            [
                lax.ppermute(tail, axis, [(i, (i + 1) % count) for i in range(ends)]),
                cells,
                lax.ppermute(head, axis, [((i + 1) % count, i) for i in range(ends)]),
            ],
            axis=dim,
        )
    return cells


def take_face(field, d, index):
    lead = field.shape[:3]
    cube = field.reshape(lead + (VARS, ORDER, ORDER, ORDER))
    face = lax.index_in_dim(cube, index, axis=4 + d, keepdims=False)
    return face.reshape(lead + (FACE_UNKNOWNS,))


def put_face(values, d, index):
    lead = values.shape[:3]
    cube = jnp.zeros(lead + (VARS, ORDER, ORDER, ORDER), values.dtype)
    spot = (slice(None),) * (4 + d) + (index,)
    cube = cube.at[spot].set(values.reshape(lead + (VARS, ORDER, ORDER)))
    return cube.reshape(lead + (ELEMENT_UNKNOWNS,))


def face_flux(matrix, left_trace, right_trace):
    paired = jnp.concatenate([left_trace, right_trace], axis=-1)
    return jnp.einsum("abcfg,abcg->abcf", matrix, paired, precision=full_precision)


def couple_faces(field, d, w_dim, face_flags, below_trace, top_flux):
    count = field.shape[d]
    lower_trace = take_face(field, d, 0)
    upper_trace = take_face(field, d, ORDER - 1)
    lower_flux = face_flux(w_dim, below_trace, lower_trace)
    upper_flux = jnp.concatenate(
        [lax.slice_in_dim(lower_flux, 1, count, axis=d), top_flux(lower_flux, upper_trace)], axis=d
    )
    lower_open = (1 - face_flags[..., 2 * d : 2 * d + 1]).astype(jnp.float32)
    upper_open = (1 - face_flags[..., 2 * d + 1 : 2 * d + 2]).astype(jnp.float32)
    lower_part = -lower_open * lower_flux + (1.0 - lower_open) * wall_weight * lower_trace
    upper_part = upper_open * upper_flux + (1.0 - upper_open) * wall_weight * upper_trace
    return put_face(lower_part, d, 0) + put_face(upper_part, d, ORDER - 1)


def neighbour(padded, d, start, length):
    spots = []
    for axis_pos in range(3):
        if axis_pos == d:
            spots.append(slice(start, start + length))
        else:
            spots.append(slice(1, padded.shape[axis_pos] - 1))
    return padded[tuple(spots)]


def ghost_faces(field, padded, d, w_dim, w_top, face_flags):
    count = field.shape[d]
    below_trace = take_face(neighbour(padded, d, 0, count), d, ORDER - 1)
    above_top = take_face(neighbour(padded, d, count + 1, 1), d, 0)

    def top_flux(lower_flux, upper_trace):
        return face_flux(w_top, lax.slice_in_dim(upper_trace, count - 1, count, axis=d), above_top)

    return couple_faces(field, d, w_dim, face_flags, below_trace, top_flux)


def least_squares(columns, start_norm):
    count = len(columns)
    cosines = []
    sine_terms = []
    target_values = [start_norm] + [jnp.zeros((), jnp.float32) for i in range(count)]
    triangle = []
    for j in range(count):
        column = list(columns[j])
        for i in range(j):
            first_entry = column[i]
            second_entry = column[i + 1]
            column[i] = cosines[i] * first_entry + sine_terms[i] * second_entry
            column[i + 1] = -sine_terms[i] * first_entry + cosines[i] * second_entry
        radius = jnp.sqrt(column[j] * column[j] + column[j + 1] * column[j + 1])
        cosine = column[j] / radius
        sine_part = column[j + 1] / radius
        cosines.append(cosine)
        sine_terms.append(sine_part)
        column[j] = radius
        target_values[j + 1] = -sine_part * target_values[j]
        target_values[j] = cosine * target_values[j]
        triangle.append(column[: j + 1])
    weights = [None] * count
    for i in reversed(range(count)):
        running = target_values[i]
        for k in range(i + 1, count):
            running = running - triangle[k][i] * weights[k]
        weights[i] = running / triangle[i][i]
    return weights


def precond_apply(precond, vector):
    return jnp.einsum("abcij,abcj->abci", precond, vector, precision=full_precision)


def shards(flux_jacobian_factor, mass_over_timestep, face_jacobian, face_flags, right_side):
    gram_part = jnp.einsum(
        "abcki,abckj->abcij",
        flux_jacobian_factor,
        flux_jacobian_factor,
        preferred_element_type=jnp.float32,
    )
    identity = jnp.eye(ELEMENT_UNKNOWNS, dtype=jnp.float32)
    jacobian = gram_part / ELEMENT_UNKNOWNS + mass_over_timestep[..., None] * identity
    factor_lower = jnp.linalg.cholesky(jacobian)
    lower_inverse = jax.scipy.linalg.solve_triangular(
        factor_lower, jnp.broadcast_to(identity, jacobian.shape), lower=True
    )
    precond = jnp.einsum(
        "abcki,abckj->abcij", lower_inverse, lower_inverse, precision=full_precision
    )
    top_blocks = (
        passed_along(face_jacobian[0:1, :, :, 0], "gx", -1),
        passed_along(face_jacobian[:, 0:1, :, 1], "gy", -1),
        passed_along(face_jacobian[:, :, 0:1, 2], "gz", -1),
    )
    start_norm = jnp.sqrt(lax.psum(jnp.sum(right_side * right_side), ("gx", "gy", "gz")))
    krylov_basis = [right_side / start_norm]
    columns = []
    for j in range(KRYLOV):
        direction = precond_apply(precond, krylov_basis[j])
        mapped = jnp.einsum("abcij,abcj->abci", jacobian, direction, precision=full_precision)
        padded = padded_2(direction, (("gx", 0), ("gy", 1), ("gz", 2)), 1)
        for d in range(3):
            mapped = mapped + ghost_faces(
                direction, padded, d, face_jacobian[:, :, :, d], top_blocks[d], face_flags
            )
        local_dots = jnp.stack([jnp.sum(vector * mapped) for vector in krylov_basis])
        project = lax.psum(local_dots, ("gx", "gy", "gz"))
        for i in range(len(krylov_basis)):
            mapped = mapped - project[i] * krylov_basis[i]
        length = jnp.sqrt(lax.psum(jnp.sum(mapped * mapped), ("gx", "gy", "gz")))
        columns.append([project[i] for i in range(len(krylov_basis))] + [length])
        if j + 1 < KRYLOV:
            krylov_basis.append(mapped / length)
    weights = least_squares(columns, start_norm)
    combined = weights[0] * krylov_basis[0]
    for j in range(1, KRYLOV):
        combined = combined + weights[j] * krylov_basis[j]
    return precond_apply(precond, combined)


def solution(mesh):
    in_specs = (
        P("gx", "gy", "gz", None, None),
        P("gx", "gy", "gz", None),
        P("gx", "gy", "gz", None, None, None),
        P("gx", "gy", "gz", None),
        P("gx", "gy", "gz", None),
    )
    out_specs = P("gx", "gy", "gz", None)
    return jax.shard_map(shards, mesh=mesh, in_specs=in_specs, out_specs=out_specs, check_vma=False)
```

profile of v0, /device:TPU:1, one launch (start us, length us, event | category | flops | bytes accessed | tf_op | source)
XLA Modules:
  0.0 1564.7 jit_solution(18332297160623081579)
XLA Ops:
  6.0 5.4 copy.356
  17.0 93.8 %custom-call.26 = f32[1,4,2,128,128]{4,3,2,1,0:T(8,128)S(1)} custom-call(f32[1,4,2,128,128]{4,3,2,1,0:T(8,128)S(1)} %cholesky.211), custom_call_target="Cholesky" | custom-call | tf_op jit(solution)/shard_map/jit(cholesky)/cholesky | solution.py:138
  110.9 78.6 %custom-call.27 = f32[1,4,2,1,128,128]{4,5,3,2,1,0:T(8,128)S(1)} custom-call(f32[1,4,2,1,128,128]{5,4,3,2,1,0:T(8,128)S(1)} %select_bitcast_fusion.1), custom_call_target="InvertDiagBlocksLowerTriangular" | custom-call | tf_op jit(solution)/shard_map/jit(cholesky)/cholesky | solution.py:138
  197.2 94.0 %custom-call.28 = f32[1,4,2,128,128]{4,3,2,1,0:T(8,128)S(1)} custom-call(f32[1,4,2,128,128]{4,3,2,1,0:T(8,128)S(1)} %cholesky.215), custom_call_target="Cholesky" | custom-call | tf_op jit(solution)/shard_map/jit(cholesky)/cholesky | solution.py:138
  292.2 78.6 %custom-call.29 = f32[1,4,2,1,128,128]{4,5,3,2,1,0:T(8,128)S(1)} custom-call(f32[1,4,2,1,128,128]{5,4,3,2,1,0:T(8,128)S(1)} %get-tuple-element.264), custom_call_target="InvertDiagBlocksLowerTriangular" | custom-call | tf_op jit(solution)/shard_map/jit(cholesky)/cholesky | solution.py:138
  374.0 46.9 %custom-call.30 = f32[1,4,2,64,64]{4,3,2,1,0:T(8,128)S(1)} custom-call(f32[1,4,2,64,64]{4,3,2,1,0:T(8,128)S(1)} %fusion.17), custom_call_target="Cholesky" | custom-call | tf_op jit(solution)/shard_map/jit(cholesky)/cholesky | solution.py:138
  427.1 8.4 while.19
  437.0 236.9 %custom-call.31 = f32[4,2,3,128,128]{3,4,2,1,0:T(8,128)} custom-call(f32[4,2,3,128,128]{4,3,2,1,0:T(8,128)S(1)} %pad_maximum_fusion), custom_call_target="InvertDiagBlocksLowerTriangular" | custom-call | tf_op jit(solution)/shard_map/jit(_solve_triangular)/vmap(vmap())/triangular_solve | solution.py:139
  688.3 10.2 fusion
  698.5 81.4 %psum.49 = f32[]{:T(128)} all-reduce(f32[]{:T(128)} %multiply_reduce_fusion.2), channel_id=1, replica_groups=mesh['gx'=4,'gy'=16,'gz'=4] {'gx','gy','gz'}, use_global_device_ids=true, to_apply=%region_7.8 | all-reduce | flops 1 | bytes 8 | tf_op jit(solution)/shard_map/psum | solution.py:150
  780.5 5.7 fusion.108
  813.4 4.9 fusion.106
  867.2 4.9 collective-permute-start.6
  911.7 78.9 %psum.50 = f32[]{:T(128)} all-reduce(f32[]{:T(128)} %get-tuple-element.260), channel_id=1, replica_groups=mesh['gx'=4,'gy'=16,'gz'=4] {'gx','gy','gz'}, use_global_device_ids=true, to_apply=%region_9.10 | all-reduce | flops 1 | bytes 8 | tf_op jit(solution)/shard_map/psum | solution.py:162
  991.8 72.8 %psum.51 = f32[]{:T(128)} all-reduce(f32[]{:T(128)} %multiply_reduce_fusion.1), channel_id=1, replica_groups=mesh['gx'=4,'gy'=16,'gz'=4] {'gx','gy','gz'}, use_global_device_ids=true, to_apply=%region_11.12 | all-reduce | flops 1 | bytes 8 | tf_op jit(solution)/shard_map/psum | solution.py:165
  1066.0 5.7 fusion.104
  1080.1 4.9 fusion.102
  1166.2 77.7 %psum.52 = f32[2]{0:T(128)S(1)} all-reduce(f32[2]{0:T(128)S(1)} %pad_maximum_fusion.37), channel_id=1, replica_groups=mesh['gx'=4,'gy'=16,'gz'=4] {'gx','gy','gz'}, use_global_device_ids=true, to_apply=%region_14.15 | all-reduce | flops 2 | bytes 16 | tf_op jit(solution)/shard_map/psum | solution.py:162
  1246.3 72.7 %psum.53 = f32[]{:T(128)} all-reduce(f32[]{:T(128)} %get-tuple-element.257), channel_id=1, replica_groups=mesh['gx'=4,'gy'=16,'gz'=4] {'gx','gy','gz'}, use_global_device_ids=true, to_apply=%region_16.17 | all-reduce | flops 1 | bytes 8 | tf_op jit(solution)/shard_map/psum | solution.py:165
  1319.7 5.7 fusion.100
  1333.6 4.9 fusion.98
  1398.8 78.6 %psum.54 = f32[3]{0:T(128)S(1)} all-reduce(f32[3]{0:T(128)S(1)} %pad_maximum_fusion.38), channel_id=1, replica_groups=mesh['gx'=4,'gy'=16,'gz'=4] {'gx','gy','gz'}, use_global_device_ids=true, to_apply=%region_20.21 | all-reduce | flops 3 | bytes 24 | tf_op jit(solution)/shard_map/psum | solution.py:162
  1484.3 72.6 %psum.55 = f32[]{:T(128)} all-reduce(f32[]{:T(128)} %fusion.110), channel_id=1, replica_groups=mesh['gx'=4,'gy'=16,'gz'=4] {'gx','gy','gz'}, use_global_device_ids=true, to_apply=%region_22.23 | all-reduce | flops 1 | bytes 8 | tf_op jit(solution)/shard_map/psum | solution.py:165
  1557.9 5.7 fusion.96
  (426 shorter events, 330.2 us)
Async XLA Ops:
  427.1 247.0 %copy-start.8 = (f32[128,320]{0,1:T(8,128)S(1)}, f32[128,320]{0,1:T(8,128)}, u32[]{:S(2)}) copy-start(f32[128,320]{0,1:T(8,128)} %get-tuple-element.267) | copy-start | bytes 491524
  435.4 240.8 %copy-start.7 = (f32[128,320]{0,1:T(8,128)S(1)}, f32[128,320]{0,1:T(8,128)}, u32[]{:S(2)}) copy-start(f32[128,320]{0,1:T(8,128)} %get-tuple-element.266) | copy-start | bytes 491524
  786.2 61.6 %collective-permute-start = (f32[1,4,2,320]{3,1,2,0:T(4,128)S(1)}, f32[1,4,2,320]{3,1,2,0:T(4,128)}, u32[]{:S(2)}, u32[]{:S(2)}) collective-permute-start(f32[1,4,2,320]{3,1,2,0:T(4,128)S(1)} %bitcast.397), channel_id=1, source_target_pairs={{0,64},{64,128},{128,192},{1,65},{65,129},{129,193},{2,66},{66,130... | collective-permute-start | bytes 30728 | tf_op jit(solution)/shard_map/ppermute | solution.py:29
  788.1 65.2 %collective-permute-start.1 = (f32[1,4,2,320]{3,1,2,0:T(4,128)S(1)}, f32[1,4,2,320]{3,1,2,0:T(4,128)}, u32[]{:S(2)}, u32[]{:S(2)}) collective-permute-start(f32[1,4,2,320]{3,1,2,0:T(4,128)S(1)} %bitcast.398), channel_id=1, source_target_pairs={{64,0},{128,64},{192,128},{65,1},{129,65},{193,129},{66,2},{130,66... | collective-permute-start | bytes 30728 | tf_op jit(solution)/shard_map/ppermute | solution.py:31
  790.3 117.2 %collective-permute-start.2 = (f32[1,4,2,80,160]{4,3,2,1,0:T(8,128)}, f32[1,4,2,80,160]{4,3,2,1,0:T(8,128)S(1)}, u32[]{:S(2)}, u32[]{:S(2)}) collective-permute-start(f32[1,4,2,80,160]{4,3,2,1,0:T(8,128)} %slice_bitcast_fusion.2), channel_id=1, source_target_pairs={{64,0},{128,64},{192,128},{65,1},{129,65},{193,129},{66,2},{130,66... | collective-permute-start | bytes 1228808 | tf_op jit(solution)/shard_map/ppermute | solution.py:18
  792.3 103.3 %collective-permute-start.5 = (f32[1,1,2,80,160]{4,3,2,1,0:T(8,128)}, f32[1,1,2,80,160]{4,3,2,1,0:T(8,128)S(1)}, u32[]{:S(2)}, u32[]{:S(2)}) collective-permute-start(f32[1,1,2,80,160]{4,3,2,1,0:T(8,128)} %slice_bitcast_fusion.16), channel_id=1, source_target_pairs={{4,0},{8,4},{12,8},{16,12},{20,16},{24,20},{28,24},{32,28},{36,32}... | collective-permute-start | bytes 307208 | tf_op jit(solution)/shard_map/ppermute | solution.py:18
  795.9 107.2 %collective-permute-start.8 = (f32[1,4,1,80,160]{4,3,1,2,0:T(8,128)}, f32[1,4,1,80,160]{4,3,1,2,0:T(8,128)S(1)}, u32[]{:S(2)}, u32[]{:S(2)}) collective-permute-start(f32[1,4,1,80,160]{4,3,1,2,0:T(8,128)} %slice_bitcast_fusion.11), channel_id=1, source_target_pairs={{1,0},{2,1},{3,2},{5,4},{6,5},{7,6},{9,8},{10,9},{11,10},{13,12},{... | collective-permute-start | bytes 614408 | tf_op jit(solution)/shard_map/ppermute | solution.py:18
  857.6 7.6 collective-permute-start.3
  860.4 5.4 collective-permute-start.4
  867.2 11.3 collective-permute-start.6
  875.7 16.5 %collective-permute-start.7 = (f32[3,6,1,320]{3,1,2,0:T(8,128)}, f32[3,6,1,320]{3,1,2,0:T(8,128)}, u32[]{:S(2)}, u32[]{:S(2)}) collective-permute-start(f32[3,6,1,320]{3,1,2,0:T(8,128)} %get-tuple-element.287), channel_id=1, source_target_pairs={{1,0},{2,1},{3,2},{5,4},{6,5},{7,6},{9,8},{10,9},{11,10},{13,12},{... | collective-permute-start | bytes 69128 | tf_op jit(solution)/shard_map/ppermute | solution.py:31
  1072.3 28.7 %collective-permute-start.9 = (f32[1,4,2,320]{3,1,2,0:T(4,128)}, f32[1,4,2,320]{3,1,2,0:T(4,128)}, u32[]{:S(2)}, u32[]{:S(2)}) collective-permute-start(f32[1,4,2,320]{3,1,2,0:T(4,128)} %bitcast.312.clone.2), channel_id=1, source_target_pairs={{0,64},{64,128},{128,192},{1,65},{65,129},{129,193},{2,66},{66,130... | collective-permute-start | bytes 30728 | tf_op jit(solution)/shard_map/ppermute | solution.py:29
  1075.5 31.8 %collective-permute-start.10 = (f32[1,4,2,320]{3,1,2,0:T(4,128)}, f32[1,4,2,320]{3,1,2,0:T(4,128)}, u32[]{:S(2)}, u32[]{:S(2)}) collective-permute-start(f32[1,4,2,320]{3,1,2,0:T(4,128)} %bitcast.312.clone.2), channel_id=1, source_target_pairs={{64,0},{128,64},{192,128},{65,1},{129,65},{193,129},{66,2},{130,66... | collective-permute-start | bytes 30728 | tf_op jit(solution)/shard_map/ppermute | solution.py:31
  1115.7 9.2 collective-permute-start.11
  1119.4 5.5 collective-permute-start.12
  1126.3 9.2 collective-permute-start.13
  1134.0 23.4 %collective-permute-start.14 = (f32[3,6,1,320]{3,1,2,0:T(8,128)}, f32[3,6,1,320]{3,1,2,0:T(8,128)}, u32[]{:S(2)}, u32[]{:S(2)}) collective-permute-start(f32[3,6,1,320]{3,1,2,0:T(8,128)} %get-tuple-element.285), channel_id=1, source_target_pairs={{1,0},{2,1},{3,2},{5,4},{6,5},{7,6},{9,8},{10,9},{11,10},{13,12},{... | collective-permute-start | bytes 69128 | tf_op jit(solution)/shard_map/ppermute | solution.py:31
  1326.0 28.9 %collective-permute-start.15 = (f32[1,4,2,320]{3,1,2,0:T(4,128)}, f32[1,4,2,320]{3,1,2,0:T(4,128)}, u32[]{:S(2)}, u32[]{:S(2)}) collective-permute-start(f32[1,4,2,320]{3,1,2,0:T(4,128)} %bitcast.309.clone.2), channel_id=1, source_target_pairs={{0,64},{64,128},{128,192},{1,65},{65,129},{129,193},{2,66},{66,130... | collective-permute-start | bytes 30728 | tf_op jit(solution)/shard_map/ppermute | solution.py:29
  1329.2 32.0 %collective-permute-start.16 = (f32[1,4,2,320]{3,1,2,0:T(4,128)}, f32[1,4,2,320]{3,1,2,0:T(4,128)}, u32[]{:S(2)}, u32[]{:S(2)}) collective-permute-start(f32[1,4,2,320]{3,1,2,0:T(4,128)} %bitcast.309.clone.2), channel_id=1, source_target_pairs={{64,0},{128,64},{192,128},{65,1},{129,65},{193,129},{66,2},{130,66... | collective-permute-start | bytes 30728 | tf_op jit(solution)/shard_map/ppermute | solution.py:31
  1368.4 7.9 collective-permute-start.17
  1372.4 5.3 collective-permute-start.18
  1378.5 4.9 collective-permute-start.19
  1381.9 10.9 collective-permute-start.20
  1391.9 172.3 %copy-start.1 = (bf16[1,4,2,320,320]{4,3,2,1,0:T(8,128)(2,1)S(1)}, bf16[1,4,2,320,320]{4,3,2,1,0:T(8,128)(2,1)}, u32[]{:S(2)}) copy-start(bf16[1,4,2,320,320]{4,3,2,1,0:T(8,128)(2,1)} %param.41) | copy-start | bytes 4915204
  (24 other events, 642.3 us)
where the time goes:
time: 1580 us; the launch traced here: 1560 us
  other arithmetic  709 us (45%)
  blocking collectives  535 us (34%)
  local copies, waits for them, and re-layouts  171 us (11%)
  matrix products  87.4 us (6%)
  starting transfers between devices  47.4 us (3%)
    another operation x14, other arithmetic, shards(): factor_lower = jnp.linalg.cholesky(jacobian)  394 us
    another operation x8, other arithmetic, shards(): jax.scipy.linalg.solve_triangular(factor_lower, jnp.broadcast_to(identity...  241 us
    psum x3, blocking collectives, shards(): project = lax.psum(local_dots, ('gx', 'gy', 'gz'))  235 us
    psum x3, blocking collectives, shards(): length = jnp.sqrt(lax.psum(jnp.sum(mapped * mapped), ('gx', 'gy', 'gz')))  218 us
    psum x1, blocking collectives, shards(): lax.psum(jnp.sum(right_side * right_side), ('gx', 'gy', 'gz'))  81.4 us
    another operation x48, local copies, waits for them, and re-layouts, take_face(): return face.reshape(lead + (FACE_UNKNOWNS,))  43.4 us
  transfers between devices with their start and end apart: 21, of which 1 were waited for; matrix products, arithmetic and copies ran while one was open for 13% of the time, Pallas kernels for 0%

commit v1 on v0

--- a/solution.py
+++ b/solution.py
@@ -2,6 +2,7 @@
 import jax.numpy as jnp
 from jax import lax
 from jax.sharding import PartitionSpec as P
+from jax.lax import psum
 
 VARS = 5
 ORDER = 4
@@ -10,6 +11,10 @@
 FACE_UNKNOWNS = 80
 full_precision = lax.Precision.HIGHEST
 wall_weight = 0.5
+
+
+def recast_the_counts(buf):
+    return psum(psum(buf, axis_name="gx"), axis_name=("gy", "gz"))
 
 
 def passed_along(block, axis, distance):
@@ -159,7 +164,7 @@
                 direction, padded, d, face_jacobian[:, :, :, d], top_blocks[d], face_flags
             )
         local_dots = jnp.stack([jnp.sum(vector * mapped) for vector in krylov_basis])
-        project = lax.psum(local_dots, ("gx", "gy", "gz"))
+        project = recast_the_counts(local_dots)
         for i in range(len(krylov_basis)):
             mapped = mapped - project[i] * krylov_basis[i]
         length = jnp.sqrt(lax.psum(jnp.sum(mapped * mapped), ("gx", "gy", "gz")))

time: 1580 us -> 1760 us (1.11)
  blocking collectives: 535 us -> 713 us
    psum x3 -> x6, blocking collectives: 235 us -> 400 us  [recast_the_counts(): return psum(psum(buf, axis_name='gx'), axis_name=('gy', 'gz'))]
  transfers between devices with their start and end apart: 21 -> 21, of which waited for: 1 -> 1; matrix products, arithmetic and copies ran while one was open for 13% -> 12% of each run, Pallas kernels for 0% -> 0%
where the time goes in v1:
time: 1760 us; the launch traced here: 1740 us
  blocking collectives  713 us (41%)
  other arithmetic  709 us (40%)
  local copies, waits for them, and re-layouts  171 us (10%)
  matrix products  87.4 us (5%)
  starting transfers between devices  49.1 us (3%)
    psum x6, blocking collectives, recast_the_counts(): return psum(psum(buf, axis_name='gx'), axis_name=('gy', 'gz'))  400 us
    another operation x14, other arithmetic, shards(): factor_lower = jnp.linalg.cholesky(jacobian)  394 us
    another operation x8, other arithmetic, shards(): jax.scipy.linalg.solve_triangular(factor_lower, jnp.broadcast_to(identity...  241 us
    psum x3, blocking collectives, shards(): length = jnp.sqrt(lax.psum(jnp.sum(mapped * mapped), ('gx', 'gy', 'gz')))  231 us
    psum x1, blocking collectives, shards(): lax.psum(jnp.sum(right_side * right_side), ('gx', 'gy', 'gz'))  81.4 us
    another operation x48, local copies, waits for them, and re-layouts, take_face(): return face.reshape(lead + (FACE_UNKNOWNS,))  43.4 us
  transfers between devices with their start and end apart: 21, of which 1 were waited for; matrix products, arithmetic and copies ran while one was open for 12% of the time, Pallas kernels for 0%

profile of v1, /device:TPU:1, one launch (start us, length us, event | category | flops | bytes accessed | tf_op | source)
XLA Modules:
  0.0 1744.3 jit_solution(93404782153074919)
XLA Ops:
  6.0 5.4 copy.356
  17.0 93.8 %custom-call.26 = f32[1,4,2,128,128]{4,3,2,1,0:T(8,128)S(1)} custom-call(f32[1,4,2,128,128]{4,3,2,1,0:T(8,128)S(1)} %cholesky.211), custom_call_target="Cholesky" | custom-call | tf_op jit(solution)/shard_map/jit(cholesky)/cholesky | solution.py:143
  110.9 78.6 %custom-call.27 = f32[1,4,2,1,128,128]{4,5,3,2,1,0:T(8,128)S(1)} custom-call(f32[1,4,2,1,128,128]{5,4,3,2,1,0:T(8,128)S(1)} %select_bitcast_fusion.1), custom_call_target="InvertDiagBlocksLowerTriangular" | custom-call | tf_op jit(solution)/shard_map/jit(cholesky)/cholesky | solution.py:143
  197.2 94.0 %custom-call.28 = f32[1,4,2,128,128]{4,3,2,1,0:T(8,128)S(1)} custom-call(f32[1,4,2,128,128]{4,3,2,1,0:T(8,128)S(1)} %cholesky.215), custom_call_target="Cholesky" | custom-call | tf_op jit(solution)/shard_map/jit(cholesky)/cholesky | solution.py:143
  292.2 78.6 %custom-call.29 = f32[1,4,2,1,128,128]{4,5,3,2,1,0:T(8,128)S(1)} custom-call(f32[1,4,2,1,128,128]{5,4,3,2,1,0:T(8,128)S(1)} %get-tuple-element.264), custom_call_target="InvertDiagBlocksLowerTriangular" | custom-call | tf_op jit(solution)/shard_map/jit(cholesky)/cholesky | solution.py:143
  374.0 46.9 %custom-call.30 = f32[1,4,2,64,64]{4,3,2,1,0:T(8,128)S(1)} custom-call(f32[1,4,2,64,64]{4,3,2,1,0:T(8,128)S(1)} %fusion.17), custom_call_target="Cholesky" | custom-call | tf_op jit(solution)/shard_map/jit(cholesky)/cholesky | solution.py:143
  427.1 8.4 while.19
  437.0 236.9 %custom-call.31 = f32[4,2,3,128,128]{3,4,2,1,0:T(8,128)} custom-call(f32[4,2,3,128,128]{4,3,2,1,0:T(8,128)S(1)} %pad_maximum_fusion), custom_call_target="InvertDiagBlocksLowerTriangular" | custom-call | tf_op jit(solution)/shard_map/jit(_solve_triangular)/vmap(vmap())/triangular_solve | solution.py:144
  688.3 10.2 fusion
  698.5 81.4 %psum.70 = f32[]{:T(128)} all-reduce(f32[]{:T(128)} %multiply_reduce_fusion.2), channel_id=1, replica_groups=mesh['gx'=4,'gy'=16,'gz'=4] {'gx','gy','gz'}, use_global_device_ids=true, to_apply=%region_7.8 | all-reduce | flops 1 | bytes 8 | tf_op jit(solution)/shard_map/psum | solution.py:155
  780.5 5.7 fusion.108
  911.7 11.3 psum.71
  922.9 123.9 %psum.72 = f32[]{:T(128)} all-reduce(f32[]{:T(128)} %bitcast.81), channel_id=1, replica_groups=mesh['gx'=4,'gy'=16,'gz'=4] {'gy','gz'}, use_global_device_ids=true, to_apply=%region_10.11 | all-reduce | flops 1 | bytes 8 | tf_op jit(solution)/shard_map/psum | solution.py:17
  1048.1 76.9 %psum.73 = f32[]{:T(128)} all-reduce(f32[]{:T(128)} %multiply_reduce_fusion.1), channel_id=1, replica_groups=mesh['gx'=4,'gy'=16,'gz'=4] {'gx','gy','gz'}, use_global_device_ids=true, to_apply=%region_12.13 | all-reduce | flops 1 | bytes 8 | tf_op jit(solution)/shard_map/psum | solution.py:170
  1126.4 5.7 fusion.104
  1227.4 9.5 psum.74
  1236.9 123.1 %psum.75 = f32[2]{0:T(128)S(1)} all-reduce(f32[2]{0:T(128)S(1)} %psum.74), channel_id=1, replica_groups=mesh['gx'=4,'gy'=16,'gz'=4] {'gy','gz'}, use_global_device_ids=true, to_apply=%region_16.17 | all-reduce | flops 2 | bytes 16 | tf_op jit(solution)/shard_map/psum | solution.py:17
  1362.5 77.3 %psum.76 = f32[]{:T(128)} all-reduce(f32[]{:T(128)} %get-tuple-element.257), channel_id=1, replica_groups=mesh['gx'=4,'gy'=16,'gz'=4] {'gx','gy','gz'}, use_global_device_ids=true, to_apply=%region_18.19 | all-reduce | flops 1 | bytes 8 | tf_op jit(solution)/shard_map/psum | solution.py:170
  1440.5 5.7 fusion.100
  1455.1 4.9 fusion.98
  1520.5 9.5 psum.77
  1530.0 122.5 %psum.78 = f32[3]{0:T(128)S(1)} all-reduce(f32[3]{0:T(128)S(1)} %psum.77), channel_id=1, replica_groups=mesh['gx'=4,'gy'=16,'gz'=4] {'gy','gz'}, use_global_device_ids=true, to_apply=%region_23.24 | all-reduce | flops 3 | bytes 24 | tf_op jit(solution)/shard_map/psum | solution.py:17
  1659.4 77.2 %psum.79 = f32[]{:T(128)} all-reduce(f32[]{:T(128)} %fusion.110), channel_id=1, replica_groups=mesh['gx'=4,'gy'=16,'gz'=4] {'gx','gy','gz'}, use_global_device_ids=true, to_apply=%region_25.26 | all-reduce | flops 1 | bytes 8 | tf_op jit(solution)/shard_map/psum | solution.py:170
  1737.6 5.7 fusion.96
  (429 shorter events, 346.7 us)
Async XLA Ops:
  427.1 247.0 %copy-start.8 = (f32[128,320]{0,1:T(8,128)S(1)}, f32[128,320]{0,1:T(8,128)}, u32[]{:S(2)}) copy-start(f32[128,320]{0,1:T(8,128)} %get-tuple-element.267) | copy-start | bytes 491524
  435.4 240.8 %copy-start.7 = (f32[128,320]{0,1:T(8,128)S(1)}, f32[128,320]{0,1:T(8,128)}, u32[]{:S(2)}) copy-start(f32[128,320]{0,1:T(8,128)} %get-tuple-element.266) | copy-start | bytes 491524
  786.2 61.6 %collective-permute-start = (f32[1,4,2,320]{3,1,2,0:T(4,128)S(1)}, f32[1,4,2,320]{3,1,2,0:T(4,128)}, u32[]{:S(2)}, u32[]{:S(2)}) collective-permute-start(f32[1,4,2,320]{3,1,2,0:T(4,128)S(1)} %bitcast.399), channel_id=1, source_target_pairs={{0,64},{64,128},{128,192},{1,65},{65,129},{129,193},{2,66},{66,130... | collective-permute-start | bytes 30728 | tf_op jit(solution)/shard_map/ppermute | solution.py:34
  788.1 65.2 %collective-permute-start.1 = (f32[1,4,2,320]{3,1,2,0:T(4,128)S(1)}, f32[1,4,2,320]{3,1,2,0:T(4,128)}, u32[]{:S(2)}, u32[]{:S(2)}) collective-permute-start(f32[1,4,2,320]{3,1,2,0:T(4,128)S(1)} %bitcast.400), channel_id=1, source_target_pairs={{64,0},{128,64},{192,128},{65,1},{129,65},{193,129},{66,2},{130,66... | collective-permute-start | bytes 30728 | tf_op jit(solution)/shard_map/ppermute | solution.py:36
  790.3 117.2 %collective-permute-start.2 = (f32[1,4,2,80,160]{4,3,2,1,0:T(8,128)}, f32[1,4,2,80,160]{4,3,2,1,0:T(8,128)S(1)}, u32[]{:S(2)}, u32[]{:S(2)}) collective-permute-start(f32[1,4,2,80,160]{4,3,2,1,0:T(8,128)} %slice_bitcast_fusion.2), channel_id=1, source_target_pairs={{64,0},{128,64},{192,128},{65,1},{129,65},{193,129},{66,2},{130,66... | collective-permute-start | bytes 1228808 | tf_op jit(solution)/shard_map/ppermute | solution.py:23
  792.3 103.3 %collective-permute-start.5 = (f32[1,1,2,80,160]{4,3,2,1,0:T(8,128)}, f32[1,1,2,80,160]{4,3,2,1,0:T(8,128)S(1)}, u32[]{:S(2)}, u32[]{:S(2)}) collective-permute-start(f32[1,1,2,80,160]{4,3,2,1,0:T(8,128)} %slice_bitcast_fusion.16), channel_id=1, source_target_pairs={{4,0},{8,4},{12,8},{16,12},{20,16},{24,20},{28,24},{32,28},{36,32}... | collective-permute-start | bytes 307208 | tf_op jit(solution)/shard_map/ppermute | solution.py:23
  795.9 107.2 %collective-permute-start.8 = (f32[1,4,1,80,160]{4,3,1,2,0:T(8,128)}, f32[1,4,1,80,160]{4,3,1,2,0:T(8,128)S(1)}, u32[]{:S(2)}, u32[]{:S(2)}) collective-permute-start(f32[1,4,1,80,160]{4,3,1,2,0:T(8,128)} %slice_bitcast_fusion.11), channel_id=1, source_target_pairs={{1,0},{2,1},{3,2},{5,4},{6,5},{7,6},{9,8},{10,9},{11,10},{13,12},{... | collective-permute-start | bytes 614408 | tf_op jit(solution)/shard_map/ppermute | solution.py:23
  857.6 7.6 collective-permute-start.3
  860.4 5.4 collective-permute-start.4
  867.2 11.3 collective-permute-start.6
  875.7 16.5 collective-permute-start.7
  1132.7 29.3 %collective-permute-start.9 = (f32[1,4,2,320]{3,1,2,0:T(4,128)}, f32[1,4,2,320]{3,1,2,0:T(4,128)}, u32[]{:S(2)}, u32[]{:S(2)}) collective-permute-start(f32[1,4,2,320]{3,1,2,0:T(4,128)} %bitcast.314.clone.2), channel_id=1, source_target_pairs={{0,64},{64,128},{128,192},{1,65},{65,129},{129,193},{2,66},{66,130... | collective-permute-start | bytes 30728 | tf_op jit(solution)/shard_map/ppermute | solution.py:34
  1136.5 31.8 %collective-permute-start.10 = (f32[1,4,2,320]{3,1,2,0:T(4,128)}, f32[1,4,2,320]{3,1,2,0:T(4,128)}, u32[]{:S(2)}, u32[]{:S(2)}) collective-permute-start(f32[1,4,2,320]{3,1,2,0:T(4,128)} %bitcast.314.clone.2), channel_id=1, source_target_pairs={{64,0},{128,64},{192,128},{65,1},{129,65},{193,129},{66,2},{130,66... | collective-permute-start | bytes 30728 | tf_op jit(solution)/shard_map/ppermute | solution.py:36
  1176.7 9.9 collective-permute-start.11
  1181.1 5.5 collective-permute-start.12
  1188.1 8.6 collective-permute-start.13
  1195.3 23.4 %collective-permute-start.14 = (f32[3,6,1,320]{3,1,2,0:T(8,128)}, f32[3,6,1,320]{3,1,2,0:T(8,128)}, u32[]{:S(2)}, u32[]{:S(2)}) collective-permute-start(f32[3,6,1,320]{3,1,2,0:T(8,128)} %get-tuple-element.285), channel_id=1, source_target_pairs={{1,0},{2,1},{3,2},{5,4},{6,5},{7,6},{9,8},{10,9},{11,10},{13,12},{... | collective-permute-start | bytes 69128 | tf_op jit(solution)/shard_map/ppermute | solution.py:36
  1446.8 29.5 %collective-permute-start.15 = (f32[1,4,2,320]{3,1,2,0:T(4,128)}, f32[1,4,2,320]{3,1,2,0:T(4,128)}, u32[]{:S(2)}, u32[]{:S(2)}) collective-permute-start(f32[1,4,2,320]{3,1,2,0:T(4,128)} %bitcast.311.clone.2), channel_id=1, source_target_pairs={{0,64},{64,128},{128,192},{1,65},{65,129},{129,193},{2,66},{66,130... | collective-permute-start | bytes 30728 | tf_op jit(solution)/shard_map/ppermute | solution.py:34
  1450.7 32.0 %collective-permute-start.16 = (f32[1,4,2,320]{3,1,2,0:T(4,128)}, f32[1,4,2,320]{3,1,2,0:T(4,128)}, u32[]{:S(2)}, u32[]{:S(2)}) collective-permute-start(f32[1,4,2,320]{3,1,2,0:T(4,128)} %bitcast.311.clone.2), channel_id=1, source_target_pairs={{64,0},{128,64},{192,128},{65,1},{129,65},{193,129},{66,2},{130,66... | collective-permute-start | bytes 30728 | tf_op jit(solution)/shard_map/ppermute | solution.py:36
  1489.8 8.2 collective-permute-start.17
  1494.2 5.3 collective-permute-start.18
  1500.3 4.9 collective-permute-start.19
  1503.6 10.9 collective-permute-start.20
  1513.7 230.2 %copy-start.1 = (bf16[1,4,2,320,320]{4,3,2,1,0:T(8,128)(2,1)S(1)}, bf16[1,4,2,320,320]{4,3,2,1,0:T(8,128)(2,1)}, u32[]{:S(2)}) copy-start(bf16[1,4,2,320,320]{4,3,2,1,0:T(8,128)(2,1)} %param.41) | copy-start | bytes 4915204
  (24 other events, 646.5 us)
